TPU v7x, 32 devices: a whole 2x2x4 slice. The times are simulated.
32 devices in a mesh: ctx: 8 (over z, x), head: 4 (over y, core).
Axes of the slice: x: 2, y: 2, z: 4, core: 2. Of those that a mesh axis runs over, the one named last changes fastest.
Arguments:
- queries: bfloat16 [16384, 128], P(('ctx', 'head')), may hold values from -6 to 6
- keys: bfloat16 [16384, 128], P(('ctx', 'head')), may hold values from -0.0625 to 0.0625
- values: bfloat16 [16384, 4096], P('ctx', 'head'), may hold values from -6 to 6
- tier_weight_rows: int32 [8, 16384], P(None, 'ctx'), may hold values from 0 to 15
- level_table: float32 [16, 32], P(None, 'head'), may hold values from 0.1 to 10
Outputs:
- mixed: bfloat16 [16384, 4096], P('ctx', 'head')
All inputs are finite; a program needn't handle non-finite values.
Results may differ from a plain program's by a relative error of at most 0.0049.
Values may be sent and summed in bfloat16 or wider, within the bound.
No kernel may reach another device: no remote copies, remote signals or barrier semaphores. Data moves between devices by JAX's collectives and lax.ppermute only.
A program may use at most 192 MiB of HBM per device.

v0:
```python
import jax
import jax.numpy as jnp
from jax import lax
from jax.sharding import PartitionSpec as P

GROUP = 128


def swapped(value, axis, distance):
    mask = 2**distance
    pairs = [(source, source ^ mask) for source in range(lax.axis_size(axis))]
    return lax.ppermute(value, axis, pairs)


def local(queries, keys, values, tier_weight_rows, level_table):
    q_whole, k_whole = (
        lax.all_gather(queries, "head", axis=0, tiled=True),
        lax.all_gather(keys, "head", axis=0, tiled=True),
    )
    tok_rows = values.shape[0]
    columns = values.shape[1]
    head_count = level_table.shape[1]
    head_width = columns // head_count
    key_width = q_whole.shape[1]
    local_bits = (tok_rows // GROUP).bit_length() - 1
    context_exponent = lax.axis_size("ctx").bit_length() - 1
    classes = jnp.arange(level_table.shape[0], dtype=jnp.int32)
    onehot = (tier_weight_rows[:, :, None] == classes[None, None, :]).astype(jnp.float32)
    weights = jnp.einsum("ltc,ch->lth", onehot, level_table, precision=lax.Precision.HIGHEST)
    share = weights / jnp.sum(weights, axis=0)
    local_state = lax.dot_general(
        k_whole, values, (((0,), (0,)), ((), ())), preferred_element_type=jnp.float32
    )
    me_index = lax.axis_index("ctx")
    subtree = local_state
    sibling_states = []
    for bit in range(context_exponent):
        incoming_partner_sums = swapped(subtree, "ctx", bit)
        mine_bit = me_index >> bit & 1
        sibling_states.append(
            jnp.where(mine_bit == 1, incoming_partner_sums, jnp.zeros_like(incoming_partner_sums))
        )
        subtree = subtree + incoming_partner_sums

    def weigh(part, level):
        scaled = part.reshape(tok_rows, head_count, head_width) * share[level][:, :, None]
        return scaled.reshape(tok_rows, columns)

    groups = tok_rows // GROUP
    q_groups = q_whole.reshape(groups, GROUP, key_width)
    k_groups = k_whole.reshape(groups, GROUP, key_width)
    scores = jnp.einsum("nik,njk->nij", q_groups, k_groups, preferred_element_type=jnp.float32)
    causal = jnp.tril(jnp.ones((GROUP, GROUP), dtype=bool))
    scores = jnp.where(causal[None], scores, 0.0).astype(jnp.bfloat16)
    near = jnp.einsum(
        "nij,njc->nic",
        scores,
        values.reshape(groups, GROUP, columns),
        preferred_element_type=jnp.float32,
    )
    total = weigh(near.reshape(tok_rows, columns), 0)
    for level in range(1, local_bits + 1):
        half = GROUP * 2 ** (level - 1)
        blocks = tok_rows // (2 * half)
        grouped_probe_matrix = k_whole.reshape(blocks, 2, half, key_width)
        grouped_content_matrix = values.reshape(blocks, 2, half, columns)
        query_blocked = q_whole.reshape(blocks, 2, half, key_width)
        cumulative_memory = jnp.einsum(
            "bsk,bsc->bkc",
            grouped_probe_matrix[:, 0],
            grouped_content_matrix[:, 0],
            preferred_element_type=jnp.float32,
        )
        cumulative_memory = cumulative_memory.astype(jnp.bfloat16)
        upper_half_branch = jnp.einsum(
            "bsk,bkc->bsc",
            query_blocked[:, 1],
            cumulative_memory,
            preferred_element_type=jnp.float32,
        )
        part = jnp.stack([jnp.zeros_like(upper_half_branch), upper_half_branch], axis=1).reshape(
            tok_rows, columns
        )
        total = total + weigh(part, level)
    for bit in range(context_exponent):
        cumulative_memory = sibling_states[bit].astype(jnp.bfloat16)
        part = jnp.dot(q_whole, cumulative_memory, preferred_element_type=jnp.float32)
        total = total + weigh(part, 1 + local_bits + bit)
    return total.astype(jnp.bfloat16)


def solution(mesh):
    placed = (
        P(("ctx", "head"), None),
        P(("ctx", "head"), None),
        P("ctx", "head"),
        P(None, "ctx"),
        P(None, "head"),
    )
    return jax.shard_map(
        local, mesh=mesh, in_specs=placed, out_specs=P("ctx", "head"), check_vma=False
    )
```

profile of v0, /device:TPU:0, one launch (start us, length us, event | category | flops | bytes accessed | tf_op | source)
XLA Modules:
  0.0 162.7 jit_solution(10967841442434719350)
XLA Ops:
  0.0 9.0 %all_gather.7 = bf16[2048,128]{1,0:T(8,128)(2,1)S(1)} all-gather(bf16[512,128]{1,0:T(8,128)(2,1)} %param.6), channel_id=1, replica_groups=mesh['ctx'=8,'head'=4] {'head'}, dimensions={0}, use_global_device_ids=true | all-gather | bytes 655360 | tf_op jit(solution)/shard_map/all_gather | solution.py:18
  9.0 2.9 %fusion.36 = f32[128,1024]{1,0:T(8,128)S(1)} fusion(bf16[2048,128]{1,0:T(8,128)(2,1)S(1)} %all_gather.7, bf16[2048,1024]{1,0:T(8,128)(2,1)} %param.7), kind=kOutput, calls=%fused_computation.75 | convolution fusion | flops 536870912 | bytes 5242880 | tf_op jit(solution)/shard_map/dot_general | solution.py:31
  12.0 1.6 collective-permute-start
  13.5 7.2 %all_gather.6 = bf16[2048,128]{1,0:T(8,128)(2,1)S(1)} all-gather(bf16[512,128]{1,0:T(8,128)(2,1)} %param.5), channel_id=1, replica_groups=mesh['ctx'=8,'head'=4] {'head'}, dimensions={0}, use_global_device_ids=true | all-gather | bytes 655360 | tf_op jit(solution)/shard_map/all_gather | solution.py:17
  22.9 4.7 %convolution_bitcast_fusion.2 = f32[4,1,256,1024]{3,2,1,0:T(8,128)} fusion(bf16[4,2,256,1024]{3,2,1,0:T(8,128)(2,1)} %bitcast.185, bf16[4,2,256,128]{3,2,1,0:T(8,128)(2,1)S(1)} %bitcast.200, bf16[4,2,256,128]{3,2,1,0:T(8,128)(2,1)S(1)} %bitcast.195), kind=kOutput, calls=%fused_computation.18 | convolution fusion | flops 537395200 | bytes 6815744 | tf_op jit(solution)/shard_map/bsk,bkc->bsc/dot_general | solution.py:75
  27.6 4.6 %convolution_bitcast_fusion.1 = f32[2,1,512,1024]{3,2,1,0:T(8,128)} fusion(bf16[2,2,512,1024]{3,2,1,0:T(8,128)(2,1)} %bitcast.186, bf16[2,2,512,128]{3,2,1,0:T(8,128)(2,1)S(1)} %bitcast.201, bf16[2,2,512,128]{3,2,1,0:T(8,128)(2,1)S(1)} %bitcast.196), kind=kOutput, calls=%fused_computation.17 | convolution fusion | flops 537133056 | bytes 6815744 | tf_op jit(solution)/shard_map/bsk,bkc->bsc/dot_general | solution.py:75
  32.2 4.7 %convolution_bitcast_fusion = f32[1,1,1024,1024]{3,2,1,0:T(8,128)} fusion(bf16[1,2,1024,1024]{3,2,1,0:T(8,128)(2,1)} %bitcast.187, bf16[1,2,1024,128]{3,2,1,0:T(8,128)(2,1)S(1)} %bitcast.202, bf16[1,2,1024,128]{3,2,1,0:T(8,128)(2,1)S(1)} %bitcast.197), kind=kOutput, calls=%fused_computation.16 | convolution fusion | flops 537001984 | bytes 6815744 | tf_op jit(solution)/shard_map/bsk,bkc->bsc/dot_general | solution.py:75
  36.9 7.0 %fusion.16 = f32[16,128,1024]{2,1,0:T(8,128)} fusion(bf16[16,128,1024]{2,1,0:T(8,128)(2,1)} %bitcast.188, bf16[16,128,128]{2,1,0:T(8,128)(2,1)S(1)} %bitcast.198, bf16[16,128,128]{2,1,0:T(8,128)(2,1)S(1)} %bitcast.203, pred[128,128]{1,0:T(8,128)(4,1)S(1)} %iota_compare_fusion.2), kind=kOutput, calls=%fused_computation.33 | convolution fusion | flops 604504064 | bytes 13647872 | tf_op jit(solution)/shard_map/nij,njc->nic/dot_general | solution.py:55
  43.9 1.6 %collective-permute-start.1 = (f32[128,1024]{1,0:T(8,128)S(1)}, f32[128,1024]{1,0:T(8,128)S(1)}, u32[]{:S(2)}, u32[]{:S(2)}) collective-permute-start(f32[128,1024]{1,0:T(8,128)S(1)} %add.40), channel_id=1, source_target_pairs={{0,8},{4,12},{8,0},{12,4},{16,24},{20,28},{24,16},{28,20},{1,9},{5... | collective-permute-start | bytes 1572872 | tf_op jit(solution)/shard_map/ppermute | solution.py:12
  45.6 4.9 %convolution_bitcast_fusion.3 = f32[8,1,128,1024]{3,2,1,0:T(8,128)} fusion(bf16[8,2,128,1024]{3,2,1,0:T(8,128)(2,1)} %bitcast.189, bf16[8,2,128,128]{3,2,1,0:T(8,128)(2,1)S(1)} %bitcast.204, bf16[8,2,128,128]{3,2,1,0:T(8,128)(2,1)S(1)} %bitcast.199), kind=kOutput, calls=%fused_computation.19 | convolution fusion | flops 537919488 | bytes 6815744 | tf_op jit(solution)/shard_map/bsk,bkc->bsc/dot_general | solution.py:75
  50.4 6.6 %stack.25.clone = f32[8,2,128,1024]{3,2,1,0:T(8,128)} pad(f32[8,1,128,1024]{3,2,1,0:T(8,128)} %convolution_bitcast_fusion.3, f32[]{:T(128)} %constant.6.clone.1), padding=0_0x1_0x0_0x0_0 | pad | bytes 12582916 | tf_op jit(solution)/shard_map/stack | solution.py:81
  57.0 9.2 %copy.12 = f32[2048,1024]{0,1:T(8,128)} copy(f32[2048,1024]{1,0:T(8,128)} %bitcast.192) | data formatting | bytes 16777216 | tf_op jit(solution)/shard_map/reshape;reshape | solution.py:46
  66.2 6.6 %stack.27.clone = f32[4,2,256,1024]{3,2,1,0:T(8,128)} pad(f32[4,1,256,1024]{3,2,1,0:T(8,128)} %convolution_bitcast_fusion.2, f32[]{:T(128)} %constant.6.clone.1), padding=0_0x1_0x0_0x0_0 | pad | bytes 12582916 | tf_op jit(solution)/shard_map/stack | solution.py:81
  72.8 9.2 %copy.15 = f32[2048,1024]{0,1:T(8,128)} copy(f32[2048,1024]{1,0:T(8,128)} %bitcast.193) | data formatting | bytes 16777216 | tf_op jit(solution)/shard_map/reshape;reshape | solution.py:46
  82.0 6.6 %stack.29.clone = f32[2,2,512,1024]{3,2,1,0:T(8,128)} pad(f32[2,1,512,1024]{3,2,1,0:T(8,128)} %convolution_bitcast_fusion.1, f32[]{:T(128)} %constant.6.clone.1), padding=0_0x1_0x0_0x0_0 | pad | bytes 12582916 | tf_op jit(solution)/shard_map/stack | solution.py:81
  88.5 9.2 %copy.18 = f32[2048,1024]{0,1:T(8,128)} copy(f32[2048,1024]{1,0:T(8,128)} %bitcast.194) | data formatting | bytes 16777216 | tf_op jit(solution)/shard_map/reshape;reshape | solution.py:46
  97.7 6.5 %stack.31 = f32[1,2,1024,1024]{3,2,1,0:T(8,128)} pad(f32[1,1,1024,1024]{3,2,1,0:T(8,128)} %convolution_bitcast_fusion, f32[]{:T(128)} %constant.6.clone.1), padding=0_0x1_0x0_0x0_0 | pad | bytes 12582916 | tf_op jit(solution)/shard_map/stack | solution.py:81
  104.3 9.2 %copy.19 = f32[2048,1024]{0,1:T(8,128)} copy(f32[2048,1024]{1,0:T(8,128)} %bitcast.191) | data formatting | bytes 16777216 | tf_op jit(solution)/shard_map/reshape;reshape | solution.py:46
  113.5 9.2 %copy.9 = f32[2048,1024]{0,1:T(8,128)} copy(f32[2048,1024]{1,0:T(8,128)} %bitcast.190) | data formatting | bytes 16777216 | tf_op jit(solution)/shard_map/reshape;reshape | solution.py:46
  122.7 1.3 fusion.22
  124.1 2.6 %collective-permute-start.2 = (bf16[128,1024]{1,0:T(8,128)(2,1)S(1)}, bf16[128,1024]{1,0:T(8,128)(2,1)}, u32[]{:S(2)}, u32[]{:S(2)}) collective-permute-start(bf16[128,1024]{1,0:T(8,128)(2,1)S(1)} %add.42), channel_id=1, source_target_pairs={{0,16},{4,20},{8,24},{12,28},{16,0},{20,4},{24,8},{28,12},{1,17},{... | collective-permute-start | bytes 786440 | tf_op jit(solution)/shard_map/ppermute | solution.py:12
  128.0 10.9 %collective-permute-done.2 = bf16[128,1024]{1,0:T(8,128)(2,1)} collective-permute-done((bf16[128,1024]{1,0:T(8,128)(2,1)S(1)}, bf16[128,1024]{1,0:T(8,128)(2,1)}, u32[]{:S(2)}, u32[]{:S(2)}) %collective-permute-start.2) | collective-permute-done | bytes 262176 | tf_op jit(solution)/shard_map/ppermute | solution.py:12
  139.0 17.3 %fusion.1 = bf16[2048,1024]{0,1:T(8,128)(2,1)} fusion(f32[1024,2048]{1,0:T(8,128)S(1)} %fusion.23, f32[1024,2048]{1,0:T(8,128)S(1)} %fusion.22, f32[2048,1024]{0,1:T(8,128)} %copy.19, f32[2048,1024]{0,1:T(8,128)} %copy.18, f32[2048,1024]{0,1:T(8,128)} %copy.15, f32[2048,1024]{0,1:T(8,128)} %copy.12, f32[2048,1024]{0,1:T(8,128)} %copy.9, ...), kind=kOutput, calls=%fused_computation.2 | convolution fusion | flops 570556416 | bytes 64225280 | tf_op jit(solution)/shard_map/dot_general | solution.py:87
  156.3 6.4 %copy.20 = bf16[2048,1024]{1,0:T(8,128)(2,1)} copy(bf16[2048,1024]{0,1:T(8,128)(2,1)} %fusion.1) | data formatting | bytes 8388608 | tf_op jit(solution)/shard_map/convert_element_type | solution.py:89
  (13 shorter events, 3.6 us)
Async XLA Ops:
  0.0 20.7 %copy-start = (f32[16,8]{0,1:T(8,128)S(1)}, f32[16,8]{0,1:T(8,128)}, u32[]{:S(2)}) copy-start(f32[16,8]{0,1:T(8,128)} %param.9) | copy-start | bytes 1540
  12.0 31.9 %collective-permute-start = (f32[128,1024]{1,0:T(8,128)S(1)}, f32[128,1024]{1,0:T(8,128)S(1)}, u32[]{:S(2)}, u32[]{:S(2)}) collective-permute-start(f32[128,1024]{1,0:T(8,128)S(1)} %fusion.36), channel_id=1, source_target_pairs={{0,4},{4,0},{8,12},{12,8},{16,20},{20,16},{24,28},{28,24},{1,5},{5... | collective-permute-start | bytes 1572872 | tf_op jit(solution)/shard_map/ppermute | solution.py:12
  43.9 80.1 %collective-permute-start.1 = (f32[128,1024]{1,0:T(8,128)S(1)}, f32[128,1024]{1,0:T(8,128)S(1)}, u32[]{:S(2)}, u32[]{:S(2)}) collective-permute-start(f32[128,1024]{1,0:T(8,128)S(1)} %add.40), channel_id=1, source_target_pairs={{0,8},{4,12},{8,0},{12,4},{16,24},{20,28},{24,16},{28,20},{1,9},{5... | collective-permute-start | bytes 1572872 | tf_op jit(solution)/shard_map/ppermute | solution.py:12
  124.1 14.9 %collective-permute-start.2 = (bf16[128,1024]{1,0:T(8,128)(2,1)S(1)}, bf16[128,1024]{1,0:T(8,128)(2,1)}, u32[]{:S(2)}, u32[]{:S(2)}) collective-permute-start(bf16[128,1024]{1,0:T(8,128)(2,1)S(1)} %add.42), channel_id=1, source_target_pairs={{0,16},{4,20},{8,24},{12,28},{16,0},{20,4},{24,8},{28,12},{1,17},{... | collective-permute-start | bytes 786440 | tf_op jit(solution)/shard_map/ppermute | solution.py:12
  139.0 23.7 %copy-start.1 = (f32[16,8]{0,1:T(8,128)S(1)}, f32[16,8]{0,1:T(8,128)}, u32[]{:S(2)}) copy-start(f32[16,8]{0,1:T(8,128)} %param.9) | copy-start | bytes 1540
where the time goes:
time: 164 us; the launch traced here: 163 us
  local copies, waits for them, and re-layouts  79.5 us (48%)
  matrix products  49.9 us (30%)
  blocking collectives  16.2 us (10%)
  waiting for transfers between devices  10.9 us (7%)
  starting transfers between devices  5.84 us (4%)
    another operation x5, local copies, waits for them, and re-layouts, weigh(): part.reshape(tok_rows, head_count, head_width) * share[level][:, :, None]  46.1 us
    another operation x4, local copies, waits for them, and re-layouts, local(): jnp.stack([jnp.zeros_like(upper_half_branch), upper_half_branch], axis=1)  26.2 us
    dot_general x3, matrix products, local(): jnp.dot(q_whole, cumulative_memory, preferred_element_type=jnp.float32)  19.9 us
    dot_general x4, matrix products, local(): jnp.einsum('bsk,bkc->bsc', query_blocked[:, 1], cumulative_memory, prefer...  18.8 us
    ppermute x3, waiting for transfers between devices, swapped(): return lax.ppermute(value, axis, pairs)  10.9 us
    all_gather x1, blocking collectives, local(): lax.all_gather(keys, 'head', axis=0, tiled=True)  9 us
    all_gather x1, blocking collectives, local(): lax.all_gather(queries, 'head', axis=0, tiled=True)  7.22 us
    dot_general x1, matrix products, local(): jnp.einsum('nij,njc->nic', scores, values.reshape(groups, GROUP, columns)...  6.98 us
  transfers between devices with their start and end apart: 3, of which 1 were waited for; matrix products, arithmetic and copies ran while one was open for 63% of the time, Pallas kernels for 0%

commit v1 on v0

--- a/solution.py
+++ b/solution.py
@@ -4,6 +4,19 @@
 from jax.sharding import PartitionSpec as P
 
 GROUP = 128
+
+
+def collect(x, axis, dim):
+    ways = lax.axis_size(axis)
+    up = [(d, (d + 1) % ways) for d in range(ways)]
+    down = [(d, (d - 1) % ways) for d in range(ways)]
+    earlier, later = ([x], [x])
+    for _ in range(ways // 2):
+        earlier.append(lax.ppermute(earlier[-1], axis, up))
+    for _ in range((ways - 1) // 2):
+        later.append(lax.ppermute(later[-1], axis, down))
+    line = jnp.concatenate([*earlier[::-1], *later[1:]], axis=dim)
+    return jnp.roll(line, (lax.axis_index(axis) - ways // 2) * x.shape[dim], axis=dim)
 
 
 def swapped(value, axis, distance):
@@ -14,7 +27,7 @@
 
 def local(queries, keys, values, tier_weight_rows, level_table):
     q_whole, k_whole = (
-        lax.all_gather(queries, "head", axis=0, tiled=True),
+        collect(queries, "head", 0),
         lax.all_gather(keys, "head", axis=0, tiled=True),
     )
     tok_rows = values.shape[0]

time: 164 us -> 196 us (1.20)
  matrix products: 49.9 us -> 85.6 us
  blocking collectives: 16.2 us -> 9.07 us
  other arithmetic: 0.19 us -> 3.47 us
  starting transfers between devices: 5.84 us -> 8.33 us
  waiting for transfers between devices: 10.9 us -> 8.44 us
    mul x1 -> x17, local copies, waits for them, and re-layouts: 0.84 us -> 61.4 us  [weigh(): part.reshape(tok_rows, head_count, head_width) * share[level][:, :, None]]
    another operation x5 -> x0, local copies, waits for them, and re-layouts: 46.1 us -> none  [weigh(): part.reshape(tok_rows, head_count, head_width) * share[level][:, :, None]]
    dot_general x3, matrix products: 19.9 us -> 54.7 us  [local(): jnp.dot(q_whole, cumulative_memory, preferred_element_type=jnp.float32)]
    all_gather x1 -> x0, blocking collectives: 7.22 us -> none  [local(): lax.all_gather(queries, 'head', axis=0, tiled=True)]
    another operation x4, local copies, waits for them, and re-layouts: 26.2 us -> 19 us  [local(): jnp.stack([jnp.zeros_like(upper_half_branch), upper_half_branch], axis=1)]
    convert_element_type x1 -> x0, local copies, waits for them, and re-layouts: 6.4 us -> none  [local(): return total.astype(jnp.bfloat16)]
    add x2, other arithmetic: 0.13 us -> 3.41 us  [local(): subtree = subtree + incoming_partner_sums]
    ppermute x0 -> x3, starting transfers between devices: none -> 2.62 us  [the longest x1 2 us: collect(): later.append(lax.ppermute(later[-1], axis, down))]
  transfers between devices with their start and end apart: 3 -> 6, of which waited for: 1 -> 1; matrix products, arithmetic and copies ran while one was open for 63% -> 35% of each run, Pallas kernels for 0% -> 0%
where the time goes in v1:
time: 196 us
  matrix products  85.6 us (44%)
  local copies, waits for them, and re-layouts  80.7 us (41%)
  blocking collectives  9.07 us (5%)
  waiting for transfers between devices  8.44 us (4%)
  starting transfers between devices  8.33 us (4%)
  other arithmetic  3.47 us (2%)
    mul x17, local copies, waits for them, and re-layouts, weigh(): part.reshape(tok_rows, head_count, head_width) * share[level][:, :, None]  61.4 us
    dot_general x3, matrix products, local(): jnp.dot(q_whole, cumulative_memory, preferred_element_type=jnp.float32)  54.7 us
    another operation x4, local copies, waits for them, and re-layouts, local(): jnp.stack([jnp.zeros_like(upper_half_branch), upper_half_branch], axis=1)  19 us
    dot_general x4, matrix products, local(): jnp.einsum('bsk,bkc->bsc', query_blocked[:, 1], cumulative_memory, prefer...  18.8 us
    all_gather x1, blocking collectives, local(): lax.all_gather(keys, 'head', axis=0, tiled=True)  9.07 us
    ppermute x3, waiting for transfers between devices, swapped(): return lax.ppermute(value, axis, pairs)  8.43 us
    dot_general x1, matrix products, local(): jnp.einsum('nij,njc->nic', scores, values.reshape(groups, GROUP, columns)...  7.01 us
    ppermute x3, starting transfers between devices, swapped(): return lax.ppermute(value, axis, pairs)  5.71 us
  transfers between devices with their start and end apart: 6, of which 1 were waited for; matrix products, arithmetic and copies ran while one was open for 35% of the time, Pallas kernels for 0%

profile of v1, /device:TPU:0, one launch (start us, length us, event | category | flops | bytes accessed | tf_op | source)
XLA Modules:
  0.0 195.9 jit_solution(16772380776208880471)
XLA Ops:
  2.5 9.1 %all_gather.3 = bf16[2048,128]{1,0:T(8,128)(2,1)S(1)} all-gather(bf16[512,128]{1,0:T(8,128)(2,1)} %param.6), channel_id=1, replica_groups=mesh['ctx'=8,'head'=4] {'head'}, dimensions={0}, use_global_device_ids=true | all-gather | bytes 655360 | tf_op jit(solution)/shard_map/all_gather | solution.py:31
  11.6 3.8 %fusion.36 = f32[128,1024]{1,0:T(8,128)} fusion(bf16[2048,128]{1,0:T(8,128)(2,1)S(1)} %all_gather.3, bf16[2048,1024]{1,0:T(8,128)(2,1)} %param.7), kind=kOutput, calls=%fused_computation.84 | convolution fusion | flops 536870912 | bytes 5242880 | tf_op jit(solution)/shard_map/dot_general | solution.py:44
  28.9 4.6 %convolution_bitcast_fusion.2 = f32[4,1,256,1024]{3,2,1,0:T(8,128)} fusion(bf16[4,2,256,1024]{3,2,1,0:T(8,128)(2,1)} %bitcast.198, bf16[4,2,256,128]{3,2,1,0:T(8,128)(2,1)S(1)} %bitcast.216, bf16[4,2,256,128]{3,2,1,0:T(8,128)(2,1)S(1)} %bitcast.203), kind=kOutput, calls=%fused_computation.18 | convolution fusion | flops 537395200 | bytes 6815744 | tf_op jit(solution)/shard_map/bsk,bkc->bsc/dot_general | solution.py:88
  33.5 4.6 %convolution_bitcast_fusion.1 = f32[2,1,512,1024]{3,2,1,0:T(8,128)} fusion(bf16[2,2,512,1024]{3,2,1,0:T(8,128)(2,1)} %bitcast.199, bf16[2,2,512,128]{3,2,1,0:T(8,128)(2,1)S(1)} %bitcast.217, bf16[2,2,512,128]{3,2,1,0:T(8,128)(2,1)S(1)} %bitcast.204), kind=kOutput, calls=%fused_computation.17 | convolution fusion | flops 537133056 | bytes 6815744 | tf_op jit(solution)/shard_map/bsk,bkc->bsc/dot_general | solution.py:88
  38.1 4.7 %convolution_bitcast_fusion = f32[1,1,1024,1024]{3,2,1,0:T(8,128)} fusion(bf16[1,2,1024,1024]{3,2,1,0:T(8,128)(2,1)} %bitcast.200, bf16[1,2,1024,128]{3,2,1,0:T(8,128)(2,1)S(1)} %bitcast.218, bf16[1,2,1024,128]{3,2,1,0:T(8,128)(2,1)S(1)} %bitcast.205), kind=kOutput, calls=%fused_computation.16 | convolution fusion | flops 537001984 | bytes 6815744 | tf_op jit(solution)/shard_map/bsk,bkc->bsc/dot_general | solution.py:88
  42.8 7.0 %fusion.16 = f32[16,128,1024]{2,1,0:T(8,128)} fusion(bf16[16,128,1024]{2,1,0:T(8,128)(2,1)} %bitcast.201, bf16[16,128,128]{2,1,0:T(8,128)(2,1)S(1)} %bitcast.206, bf16[16,128,128]{2,1,0:T(8,128)(2,1)S(1)} %bitcast.219, pred[128,128]{1,0:T(8,128)(4,1)S(1)} %iota_compare_fusion.2), kind=kOutput, calls=%fused_computation.33 | convolution fusion | flops 604504064 | bytes 13647872 | tf_op jit(solution)/shard_map/nij,njc->nic/dot_general | solution.py:68
  53.5 4.9 %convolution_bitcast_fusion.3 = f32[8,1,128,1024]{3,2,1,0:T(8,128)} fusion(bf16[8,2,128,1024]{3,2,1,0:T(8,128)(2,1)} %bitcast.202, bf16[8,2,128,128]{3,2,1,0:T(8,128)(2,1)S(1)} %bitcast.220, bf16[8,2,128,128]{3,2,1,0:T(8,128)(2,1)S(1)} %bitcast.207), kind=kOutput, calls=%fused_computation.19 | convolution fusion | flops 537919488 | bytes 6815744 | tf_op jit(solution)/shard_map/bsk,bkc->bsc/dot_general | solution.py:88
  58.3 6.7 %stack.25.clone = f32[8,2,128,1024]{3,2,1,0:T(8,128)} pad(f32[8,1,128,1024]{3,2,1,0:T(8,128)} %convolution_bitcast_fusion.3, f32[]{:T(128)} %constant.45.clone.1), padding=0_0x1_0x0_0x0_0 | pad | bytes 12582916 | tf_op jit(solution)/shard_map/stack | solution.py:94
  65.1 4.1 %stack.27.clone = f32[4,2,256,1024]{3,2,1,0:T(8,128)} pad(f32[4,1,256,1024]{3,2,1,0:T(8,128)S(1)} %copy-done.4, f32[]{:T(128)} %constant.45.clone.1), padding=0_0x1_0x0_0x0_0 | pad | bytes 12582916 | tf_op jit(solution)/shard_map/stack | solution.py:94
  69.2 4.1 %stack.29.clone = f32[2,2,512,1024]{3,2,1,0:T(8,128)} pad(f32[2,1,512,1024]{3,2,1,0:T(8,128)S(1)} %copy-done.3, f32[]{:T(128)} %constant.45.clone.1), padding=0_0x1_0x0_0x0_0 | pad | bytes 12582916 | tf_op jit(solution)/shard_map/stack | solution.py:94
  73.3 4.1 %stack.31 = f32[1,2,1024,1024]{3,2,1,0:T(8,128)} pad(f32[1,1,1024,1024]{3,2,1,0:T(8,128)S(1)} %copy-done.2, f32[]{:T(128)} %constant.45.clone.1), padding=0_0x1_0x0_0x0_0 | pad | bytes 12582916 | tf_op jit(solution)/shard_map/stack | solution.py:94
  77.4 4.5 %fusion.22 = f32[2048,1024]{1,0:T(8,128)} fusion(bf16[2048,128]{1,0:T(8,128)(2,1)S(1)} %constant_dynamic-slice_fusion, f32[128,1024]{1,0:T(8,128)} %collective-permute-done.3, pred[]{:T(512)S(6)} %eq.28), kind=kOutput, calls=%fused_computation.43 | convolution fusion | flops 537001984 | bytes 9437185 | tf_op jit(solution)/shard_map/dot_general | solution.py:100
  83.2 2.7 %collective-permute-start.5 = (bf16[128,1024]{1,0:T(8,128)(2,1)S(1)}, bf16[128,1024]{1,0:T(8,128)(2,1)S(1)}, u32[]{:S(2)}, u32[]{:S(2)}) collective-permute-start(bf16[128,1024]{1,0:T(8,128)(2,1)S(1)} %add.55), channel_id=1, source_target_pairs={{0,16},{4,20},{8,24},{12,28},{16,0},{20,4},{24,8},{28,12},{1,17},{... | collective-permute-start | bytes 786440 | tf_op jit(solution)/shard_map/ppermute | solution.py:25
  85.9 4.5 %fusion.23 = f32[2048,1024]{1,0:T(8,128)} fusion(bf16[2048,128]{1,0:T(8,128)(2,1)S(1)} %constant_dynamic-slice_fusion, f32[128,1024]{1,0:T(8,128)} %collective-permute-done.4, pred[]{:T(512)S(6)} %eq.29), kind=kOutput, calls=%fused_computation.44 | convolution fusion | flops 537001984 | bytes 9437185 | tf_op jit(solution)/shard_map/dot_general | solution.py:100
  90.3 8.4 %collective-permute-done.5 = bf16[128,1024]{1,0:T(8,128)(2,1)S(1)} collective-permute-done((bf16[128,1024]{1,0:T(8,128)(2,1)S(1)}, bf16[128,1024]{1,0:T(8,128)(2,1)S(1)}, u32[]{:S(2)}, u32[]{:S(2)}) %collective-permute-start.5) | collective-permute-done | bytes 262176 | tf_op jit(solution)/shard_map/ppermute | solution.py:25
  98.8 6.4 %mul.113 = f32[2048,8,128]{2,1,0:T(8,128)} broadcast(f32[2048,8]{1,0:T(8,128)S(1)} %copy-done.10), dimensions={0,1} | broadcast | bytes 8454144 | tf_op jit(solution)/shard_map/mul | solution.py:59
  105.1 6.4 %mul.117 = f32[2048,8,128]{2,1,0:T(8,128)} broadcast(f32[2048,8]{1,0:T(8,128)S(1)} %copy-done.9), dimensions={0,1} | broadcast | bytes 8454144 | tf_op jit(solution)/shard_map/mul | solution.py:59
  111.5 6.5 %mul.121 = f32[2048,8,128]{2,1,0:T(8,128)} broadcast(f32[2048,8]{1,0:T(8,128)S(1)} %copy-done.8), dimensions={0,1} | broadcast | bytes 8454144 | tf_op jit(solution)/shard_map/mul | solution.py:59
  118.0 6.4 %mul.125 = f32[2048,8,128]{2,1,0:T(8,128)} broadcast(f32[2048,8]{1,0:T(8,128)S(1)} %copy-done.7), dimensions={0,1} | broadcast | bytes 8454144 | tf_op jit(solution)/shard_map/mul | solution.py:59
  124.4 6.5 %mul.129 = f32[2048,8,128]{2,1,0:T(8,128)} broadcast(f32[2048,8]{1,0:T(8,128)S(1)} %copy-done.6), dimensions={0,1} | broadcast | bytes 8454144 | tf_op jit(solution)/shard_map/mul | solution.py:59
  130.9 6.3 %mul.133 = f32[2048,8,128]{2,1,0:T(8,128)} broadcast(f32[2048,8]{1,0:T(8,128)S(1)} %copy-done.5), dimensions={0,1} | broadcast | bytes 8454144 | tf_op jit(solution)/shard_map/mul | solution.py:59
  137.3 6.3 %mul.137 = f32[2048,8,128]{2,1,0:T(8,128)} broadcast(f32[2048,8]{1,0:T(8,128)S(1)} %copy.27), dimensions={0,1} | broadcast | bytes 8454144 | tf_op jit(solution)/shard_map/mul | solution.py:59
  143.6 6.3 %mul.109 = f32[2048,8,128]{2,1,0:T(8,128)} broadcast(f32[2048,8]{1,0:T(8,128)S(1)} %copy.14), dimensions={0,1} | broadcast | bytes 8454144 | tf_op jit(solution)/shard_map/mul | solution.py:59
  149.9 45.8 %fusion.1 = bf16[2048,1024]{1,0:T(8,128)(2,1)} fusion(f32[256,8,8,128]{3,2,1,0:T(8,128)} %bitcast.214, f32[2048,1024]{1,0:T(8,128)} %fusion.23, f32[256,8,8,128]{3,2,1,0:T(8,128)} %bitcast.213, f32[2048,1024]{1,0:T(8,128)} %fusion.22, f32[256,8,8,128]{3,2,1,0:T(8,128)} %bitcast.212, f32[256,8,8,128]{3,2,1,0:T(8,128)} %bitcast.211, ...), kind=kOutput, calls=%fused_computation.2 | convolution fusion | flops 570556416 | bytes 130809856 | tf_op jit(solution)/shard_map/dot_general | solution.py:100
  (57 shorter events, 20.9 us)
Async XLA Ops:
  0.0 16.9 %copy-start = (f32[16,8]{0,1:T(8,128)S(1)}, f32[16,8]{0,1:T(8,128)}, u32[]{:S(2)}) copy-start(f32[16,8]{0,1:T(8,128)} %param.9) | copy-start | bytes 1540
  0.0 18.2 %collective-permute-start = (bf16[512,128]{1,0:T(8,128)(2,1)}, bf16[512,128]{1,0:T(8,128)(2,1)S(1)}, u32[]{:S(2)}, u32[]{:S(2)}) collective-permute-start(bf16[512,128]{1,0:T(8,128)(2,1)} %param.5), channel_id=1, source_target_pairs={{0,1},{1,2},{2,3},{3,0},{4,5},{5,6},{6,7},{7,4},{8,9},{9,10},{10,1... | collective-permute-start | bytes 393224 | tf_op jit(solution)/shard_map/ppermute | solution.py:15
  0.5 28.2 %collective-permute-start.2 = (bf16[512,128]{1,0:T(8,128)(2,1)}, bf16[512,128]{1,0:T(8,128)(2,1)S(1)}, u32[]{:S(2)}, u32[]{:S(2)}) collective-permute-start(bf16[512,128]{1,0:T(8,128)(2,1)} %param.5), channel_id=1, source_target_pairs={{0,3},{1,0},{2,1},{3,2},{4,7},{5,4},{6,5},{7,6},{8,11},{9,8},{10,9... | collective-permute-start | bytes 393224 | tf_op jit(solution)/shard_map/ppermute | solution.py:17
  11.6 17.1 %copy-start.11 = (bf16[512,128]{1,0:T(8,128)(2,1)S(1)}, bf16[512,128]{1,0:T(8,128)(2,1)}, u32[]{:S(2)}) copy-start(bf16[512,128]{1,0:T(8,128)(2,1)} %param.5) | copy-start | bytes 393220
  15.4 34.5 %collective-permute-start.3 = (f32[128,1024]{1,0:T(8,128)}, f32[128,1024]{1,0:T(8,128)}, u32[]{:S(2)}, u32[]{:S(2)}) collective-permute-start(f32[128,1024]{1,0:T(8,128)} %fusion.36), channel_id=1, source_target_pairs={{0,4},{4,0},{8,12},{12,8},{16,20},{20,16},{24,28},{28,24},{1,5},{5... | collective-permute-start | bytes 1572872 | tf_op jit(solution)/shard_map/ppermute | solution.py:25
  18.2 10.4 %collective-permute-start.1 = (bf16[512,128]{1,0:T(8,128)(2,1)S(1)}, bf16[512,128]{1,0:T(8,128)(2,1)S(1)}, u32[]{:S(2)}, u32[]{:S(2)}) collective-permute-start(bf16[512,128]{1,0:T(8,128)(2,1)S(1)} %collective-permute-done), channel_id=1, source_target_pairs={{0,1},{1,2},{2,3},{3,0},{4,5},{5,6},{6,7},{7,4},{8,9},{9,10},{10,1... | collective-permute-start | bytes 393224 | tf_op jit(solution)/shard_map/ppermute | solution.py:15
  51.9 30.0 %collective-permute-start.4 = (f32[128,1024]{1,0:T(8,128)}, f32[128,1024]{1,0:T(8,128)}, u32[]{:S(2)}, u32[]{:S(2)}) collective-permute-start(f32[128,1024]{1,0:T(8,128)} %add.53), channel_id=1, source_target_pairs={{0,8},{4,12},{8,0},{12,4},{16,24},{20,28},{24,16},{28,20},{1,9},{5... | collective-permute-start | bytes 1572872 | tf_op jit(solution)/shard_map/ppermute | solution.py:25
  58.3 6.7 %copy-start.4 = (f32[4,1,256,1024]{3,2,1,0:T(8,128)S(1)}, f32[4,1,256,1024]{3,2,1,0:T(8,128)}, u32[]{:S(2)}) copy-start(f32[4,1,256,1024]{3,2,1,0:T(8,128)} %convolution_bitcast_fusion.2) | copy-start | bytes 12582916
  65.1 4.1 %copy-start.3 = (f32[2,1,512,1024]{3,2,1,0:T(8,128)S(1)}, f32[2,1,512,1024]{3,2,1,0:T(8,128)}, u32[]{:S(2)}) copy-start(f32[2,1,512,1024]{3,2,1,0:T(8,128)} %convolution_bitcast_fusion.1) | copy-start | bytes 12582916
  69.2 4.1 %copy-start.2 = (f32[1,1,1024,1024]{3,2,1,0:T(8,128)S(1)}, f32[1,1,1024,1024]{3,2,1,0:T(8,128)}, u32[]{:S(2)}) copy-start(f32[1,1,1024,1024]{3,2,1,0:T(8,128)} %convolution_bitcast_fusion) | copy-start | bytes 12582916
  81.9 16.9 %copy-start.10 = (f32[2048,8]{1,0:T(8,128)S(1)}, f32[2048,8]{1,0:T(8,128)}, u32[]{:S(2)}) copy-start(f32[2048,8]{1,0:T(8,128)} %copy.17) | copy-start | bytes 196612
  83.2 15.6 %collective-permute-start.5 = (bf16[128,1024]{1,0:T(8,128)(2,1)S(1)}, bf16[128,1024]{1,0:T(8,128)(2,1)S(1)}, u32[]{:S(2)}, u32[]{:S(2)}) collective-permute-start(bf16[128,1024]{1,0:T(8,128)(2,1)S(1)} %add.55), channel_id=1, source_target_pairs={{0,16},{4,20},{8,24},{12,28},{16,0},{20,4},{24,8},{28,12},{1,17},{... | collective-permute-start | bytes 786440 | tf_op jit(solution)/shard_map/ppermute | solution.py:25
  90.3 14.8 %copy-start.9 = (f32[2048,8]{1,0:T(8,128)S(1)}, f32[2048,8]{1,0:T(8,128)}, u32[]{:S(2)}) copy-start(f32[2048,8]{1,0:T(8,128)} %copy.20) | copy-start | bytes 196612
  90.3 21.2 %copy-start.8 = (f32[2048,8]{1,0:T(8,128)S(1)}, f32[2048,8]{1,0:T(8,128)}, u32[]{:S(2)}) copy-start(f32[2048,8]{1,0:T(8,128)} %copy.23) | copy-start | bytes 196612
  105.1 12.9 %copy-start.7 = (f32[2048,8]{1,0:T(8,128)S(1)}, f32[2048,8]{1,0:T(8,128)}, u32[]{:S(2)}) copy-start(f32[2048,8]{1,0:T(8,128)} %copy.24) | copy-start | bytes 196612
  111.5 12.9 %copy-start.6 = (f32[2048,8]{1,0:T(8,128)S(1)}, f32[2048,8]{1,0:T(8,128)}, u32[]{:S(2)}) copy-start(f32[2048,8]{1,0:T(8,128)} %copy.25) | copy-start | bytes 196612
  118.0 12.9 %copy-start.5 = (f32[2048,8]{1,0:T(8,128)S(1)}, f32[2048,8]{1,0:T(8,128)}, u32[]{:S(2)}) copy-start(f32[2048,8]{1,0:T(8,128)} %copy.26) | copy-start | bytes 196612
  149.9 45.8 %copy-start.1 = (f32[16,8]{0,1:T(8,128)S(1)}, f32[16,8]{0,1:T(8,128)}, u32[]{:S(2)}) copy-start(f32[16,8]{0,1:T(8,128)} %param.9) | copy-start | bytes 1540
